TPU v7x, 256 devices: a whole 4x4x8 slice. The times are simulated.
256 devices in a mesh: seq: 32 (over x, y, core), head: 8 (over z).
Axes of the slice: x: 4, y: 4, z: 8, core: 2. Of those that a mesh axis runs over, the one named last changes fastest.
Arguments:
- x_in: bfloat16 [81920, 6144], P('seq', 'head'), may hold values from -6 to 6
- bc_in: bfloat16 [81920, 256], P('seq'), may hold values from -6 to 6
- gate_in: bfloat16 [81920, 6144], P('seq', 'head'), may hold values from -45 to 45
- log_decay: float32 [96, 81920], P('head', 'seq'), may hold values from -2.5 to 0, as said below
- step_size: float32 [96, 81920], P('head', 'seq'), may hold values from 0 to 0.5, as said below
- conv_x: bfloat16 [4, 6144], P(None, 'head'), may hold values from -3 to 3
- conv_bc: bfloat16 [4, 256], replicated, may hold values from -3 to 3
- skip_gain: float32 [96], P('head'), may hold values from 0.1 to 1.9
- norm_gain: float32 [6144], P('head'), may hold values from 0.5 to 1.5
Outputs:
- mamba_out: bfloat16 [81920, 6144], P('seq', 'head')
Inputs may be any that keep to these rules, and one draw needn't show every extreme that they name: `log_decay`: negative. `step_size`: positive.
All inputs are finite; a program needn't handle non-finite values.
Results may differ from a plain program's by a relative error of at most 0.0054.
Values may be sent and summed in bfloat16 or wider, within the bound.
A program may use at most 128 MiB of HBM per device.

v0:
```python
import jax
import jax.numpy as jnp
from jax import lax
from jax.sharding import PartitionSpec as P

HP = 64
NS = 128
CONV = 4
BLOCK = 256
INNER = 6144


def entering(shard, axis, join, neutral):
    place = lax.axis_index(axis)
    gathered = jax.tree.map(
        lambda a, kind: lax.all_gather(a.astype(kind), axis), shard, (jnp.bfloat16, jnp.bfloat16)
    )
    state = jax.tree.map(lambda a, e: jnp.zeros_like(a) + jnp.asarray(e, a.dtype), shard, neutral)

    def one(lap, state):
        return join(
            state,
            jax.tree.map(
                lambda a, own: lax.dynamic_index_in_dim(a, lap, 0, False).astype(own.dtype),
                gathered,
                shard,
            ),
        )

    return lax.fori_loop(0, place, one, state)


def from_behind(value, axis, steps):
    count = lax.axis_size(axis)
    leading, last = (max(0, -steps), min(count, count - steps))
    return lax.ppermute(value, axis, [(source, source + steps) for source in range(leading, last)])


def conv_silu(extended, kernel, row_count):
    running = jnp.zeros((row_count, extended.shape[1]), jnp.float32)
    for offset in range(kernel.shape[0]):
        running = running + extended[offset : offset + row_count].astype(jnp.float32) * kernel[
            offset
        ].astype(jnp.float32)
    return jax.nn.silu(running).astype(jnp.bfloat16)


def combine(earlier, later):
    return (earlier[0] + later[0], jnp.exp(later[0])[:, None, None] * earlier[1] + later[1])


def chain_state(local_decay, local_state):
    identity = (jnp.zeros_like(local_decay), jnp.zeros_like(local_state))
    prior = entering((local_decay, local_state), "seq", combine, identity)
    return prior[1]


def mamba_layer(xs_rows, bc_rows, gate_in, log_decay, step_size, skip_gain, norm_gain):
    head_count, row_count = log_decay.shape
    block_count = row_count // BLOCK
    width = head_count * HP
    causal_mask = jnp.arange(BLOCK)[:, None] >= jnp.arange(BLOCK)[None, :]
    decay_grid = log_decay.reshape(head_count, block_count, BLOCK)
    cum_inner = jnp.cumsum(decay_grid, axis=2)
    block_total = cum_inner[:, :, -1]
    block_offset = jnp.cumsum(block_total, axis=1) - block_total
    cum_rows = (cum_inner + block_offset[:, :, None]).reshape(head_count, row_count)
    local_decay = jnp.sum(block_total, axis=1)

    def advance(state_now, pieces):
        xs_blk, bc_blk, cum_decay, step_blk = pieces
        b_blk = bc_blk[:, :NS]
        c_blk = bc_blk[:, NS:]
        xs_heads = xs_blk.reshape(BLOCK, head_count, HP)
        scores = jnp.einsum("in,jn->ij", c_blk, b_blk, preferred_element_type=jnp.float32)
        gap = jnp.where(causal_mask[None], cum_decay[:, :, None] - cum_decay[:, None, :], -jnp.inf)
        weights = (scores[None] * jnp.exp(gap) * step_blk[:, None, :]).astype(jnp.bfloat16)
        intra_part = jnp.einsum(
            "hij,jhp->ihp", weights, xs_heads, preferred_element_type=jnp.float32
        )
        carried = (
            jnp.einsum(
                "in,hpn->ihp", c_blk.astype(jnp.float32), state_now, precision=lax.Precision.HIGHEST
            )
            * jnp.exp(cum_decay).T[:, :, None]
        )
        tail_factor = jnp.exp(cum_decay[:, -1:] - cum_decay) * step_blk
        weighted = (xs_heads.astype(jnp.float32) * tail_factor.T[:, :, None]).astype(jnp.bfloat16)
        update = jnp.einsum("jhp,jn->hpn", weighted, b_blk, preferred_element_type=jnp.float32)
        new_state = jnp.exp(cum_decay[:, -1])[:, None, None] * state_now + update
        mixed_rows = intra_part + carried + skip_gain[None, :, None] * xs_heads.astype(jnp.float32)
        return (new_state, mixed_rows.reshape(BLOCK, width))

    cum_blocks = cum_inner.transpose(1, 0, 2)
    step_blocks = step_size.reshape(head_count, block_count, BLOCK).transpose(1, 0, 2)
    start_state = jnp.zeros((head_count, HP, NS), jnp.float32)
    local_state, mixed_blocks = lax.scan(
        advance,
        start_state,
        (
            xs_rows.reshape(block_count, BLOCK, width),
            bc_rows.reshape(block_count, BLOCK, 2 * NS),
            cum_blocks,
            step_blocks,
        ),
    )
    incoming = chain_state(local_decay, local_state)
    c_rows = bc_rows[:, NS:].astype(jnp.float32)
    flat_state = incoming.reshape(width, NS)
    raw_correction = lax.dot_general(
        c_rows, flat_state, (((1,), (1,)), ((), ())), precision=lax.Precision.HIGHEST
    )
    correction = (
        raw_correction.reshape(row_count, head_count, HP) * jnp.exp(cum_rows).T[:, :, None]
    ).reshape(row_count, width)
    mixed_rows = mixed_blocks.reshape(row_count, width) + correction
    gated_rows = mixed_rows * jax.nn.silu(gate_in.astype(jnp.float32))
    square_sum = lax.psum(jnp.sum(gated_rows * gated_rows, axis=1), "head")
    mean_square = square_sum / INNER
    return (gated_rows * lax.rsqrt(mean_square + 1e-05)[:, None] * norm_gain).astype(jnp.bfloat16)


def per_device(x_in, bc_in, gate_in, log_decay, step_size, conv_x, conv_bc, skip_gain, norm_gain):
    tail_rows = CONV - 1
    x_prev, bc_prev = from_behind((x_in[-tail_rows:], bc_in[-tail_rows:]), "seq", 1)
    row_count = x_in.shape[0]
    xs_rows = conv_silu(jnp.concatenate([x_prev, x_in]), conv_x, row_count)
    bc_rows = conv_silu(jnp.concatenate([bc_prev, bc_in]), conv_bc, row_count)
    return mamba_layer(xs_rows, bc_rows, gate_in, log_decay, step_size, skip_gain, norm_gain)


def solution(mesh):
    in_specs = (
        P("seq", "head"),
        P("seq", None),
        P("seq", "head"),
        P("head", "seq"),
        P("head", "seq"),
        P(None, "head"),
        P(),
        P("head"),
        P("head"),
    )
    out_specs = P("seq", "head")
    return jax.shard_map(
        per_device, mesh=mesh, in_specs=in_specs, out_specs=out_specs, check_vma=False
    )
```

profile of v0, /device:TPU:30, one launch (start us, length us, event | category | flops | bytes accessed | tf_op | source)
XLA Modules:
  0.0 273.1 jit_solution(400011309588667831)
XLA Ops:
  7.3 1.9 collective-permute-start.1
  10.0 1.9 collective-permute-start
  13.7 6.8 %reduce-window.6 = f32[12,10,2,128]{3,1,2,0:T(8,128)S(1)} reduce-window(f32[12,10,2,128]{3,1,2,0:T(8,128)S(1)} %copy.42, f32[]{:T(128)} %constant.55.clone.1), window={size=1x1x1x128 pad=0_0x0_0x0_0x127_0}, to_apply=%region_0.1 | reduce-window | flops 3901440 | bytes 245764 | tf_op jit(solution)/shard_map/reduce-window
  22.3 2.5 copy.46
  24.8 2.7 multiply_convert_fusion.10
  27.5 11.0 %multiply_convert_fusion.9 = bf16[2560,768]{1,0:T(8,128)(2,1)} fusion(bf16[2560,768]{1,0:T(8,128)(2,1)} %param.13, bf16[3,768]{1,0:T(4,128)(2,1)S(1)} %collective-permute-done, f32[768]{0:T(1024)S(1)} %get-tuple-element.155, f32[768]{0:T(1024)S(1)} %get-tuple-element.156, f32[768]{0:T(1024)S(1)} %get-tuple-element.154, f32[768]{0:T(1024)S(1)} %get-tuple-element.153), kind=kLoop, calls=%fused_computation.51 | loop fusion | flops 49152000 | bytes 7881216 | tf_op jit(solution)/shard_map/convert_element_type | solution.py:45
  38.6 67.5 %while.26 = (s32[]{:T(128)}, f32[12,64,128]{2,1,0:T(8,128)S(1)}, f32[10,256,768]{2,1,0:T(8,128)}, f32[10,12,256]{2,1,0:T(8,128)S(1)}, bf16[10,256,768]{2,1,0:T(8...) while((s32[]{:T(128)}, f32[12,64,128]{2,1,0:T(8,128)S(1)}, ...), condition=%wide.region_3.4_spmd.clone, body=%wide.region_2.3_spmd.clone.sunk | while | flops 475731968 | bytes 10490800 | solution.py:97
  108.5 58.9 %all-reduce = bf16[384]{0:T(512)(128)(2,1)S(1)} all-reduce(bf16[384]{0:T(512)(128)(2,1)S(1)} %dynamic-update-slice), channel_id=2, replica_groups=mesh['seq'=32,'head'=8] {'seq'}, use_global_device_ids=true, to_apply=%add | all-reduce | flops 384 | bytes 1536
  168.3 33.3 %while.25 = (s32[]{:T(128)}, f32[12,64,128]{2,1,0:T(8,128)S(1)}, s32[]{:T(128)}, bf16[32,12]{1,0:T(8,128)(2,1)S(1)}, bf16[32,12,64,128]{3,2,1,0:T(8,128)(2,1)}, /*index=5*/s32[]{:T(128)}, s32[]{:T(128)}, s32[]{:T(128)}) while((s32[]{:T(128)}, f32[12,64,128]{2,1,0:T(8,128)S(1)}, s32[]{:T(128)}, bf16[32,12]{1,0:T(8,128)(2,1)S(1)}, ...), condition=%wide.region_6.7_spmd, body=%wide.region_5.6_spmd.sunk | while | flops 294929 | bytes 983295 | solution.py:30
  168.3 1.1 convert_add_fusion.2
  169.4 1.1 convert_add_fusion.2
  170.5 1.1 convert_add_fusion.2
  171.6 1.1 convert_add_fusion.2
  172.8 1.1 convert_add_fusion.2
  173.9 1.1 convert_add_fusion.2
  175.0 1.1 convert_add_fusion.2
  176.1 1.1 convert_add_fusion.2
  181.6 1.1 convert_add_fusion.2
  190.5 1.1 convert_add_fusion.2
  201.6 6.4 %convolution_multiply_fusion.1 = f32[2560,12,64]{0,2,1:T(8,128)} fusion(f32[12,64,128]{2,1,0:T(8,128)S(1)} %get-tuple-element.99, f32[2560,12]{0,1:T(8,128)S(1)} %exponential_bitcast_fusion.2, bf16[2560,256]{1,0:T(8,128)(2,1)} %multiply_convert_fusion.10), kind=kOutput, calls=%fused_computation.52 | convolution fusion | flops 3021864960 | bytes 9035776 | tf_op jit(solution)/shard_map/dot_general | solution.py:110
  208.0 9.1 %copy.52 = f32[2560,768]{1,0:T(8,128)} copy(f32[2560,768]{0,1:T(8,128)} %bitcast.101) | data formatting | bytes 15728640 | tf_op jit(solution)/shard_map/reshape | solution.py:115
  217.1 11.1 %multiply_reduce_fusion = (f32[2560]{0:T(1024)S(1)}, f32[2560,768]{1,0:T(8,128)}) fusion(bf16[2560,768]{1,0:T(8,128)(2,1)} %param.15, f32[2560,768]{1,0:T(8,128)} %copy.52, f32[10,256,768]{2,1,0:T(8,128)} %get-tuple-element.97), kind=kLoop, calls=%fused_computation.50 | loop fusion | flops 17692160 | bytes 27535360 | tf_op jit(solution)/shard_map/reduce_sum | solution.py:118
  228.3 32.8 %psum.7 = f32[2560]{0:T(1024)S(1)} all-reduce(f32[2560]{0:T(1024)S(1)} %get-tuple-element.185), channel_id=1, replica_groups=mesh['seq'=32,'head'=8] {'head'}, use_global_device_ids=true, to_apply=%region_9.10 | all-reduce | flops 2560 | bytes 20480 | tf_op jit(solution)/shard_map/psum | solution.py:118
  261.1 5.2 %multiply_convert_fusion.8 = bf16[2560,768]{1,0:T(8,128)(2,1)} fusion(f32[2560,768]{1,0:T(8,128)} %get-tuple-element.186, f32[768]{0:T(1024)S(1)} %copy-done.1, f32[2560]{0:T(1024)S(1)} %add_rsqrt_fusion), kind=kLoop, calls=%fused_computation.49 | loop fusion | flops 5898240 | bytes 11809792 | tf_op jit(solution)/shard_map/convert_element_type | solution.py:120
  (285 shorter events, 96.3 us)
Async XLA Ops:
  6.5 18.3 %copy-start = (bf16[2560,256]{1,0:T(8,128)(2,1)S(1)}, bf16[2560,256]{1,0:T(8,128)(2,1)}, u32[]{:S(2)}) copy-start(bf16[2560,256]{1,0:T(8,128)(2,1)} %param.14) | copy-start | bytes 3932164
  6.5 161.7 %all-gather.4.cloned.1.call-start = ((), (), s32[]{:S(2)}) async-start(), calls=%async_computation | async-start | bytes 6488064 | tf_op jit(solution)/shard_map/all_gather | solution.py:16
  7.3 17.5 %collective-permute-start.1 = (bf16[3,256]{1,0:T(4,128)(2,1)S(1)}, bf16[3,256]{1,0:T(4,128)(2,1)S(1)}, u32[]{:S(2)}, u32[]{:S(2)}) collective-permute-start(bf16[3,256]{1,0:T(4,128)(2,1)S(1)} %slice.80), channel_id=1, source_target_pairs={{0,8},{8,16},{16,24},{24,32},{32,40},{40,48},{48,56},{56,64},{64,7... | collective-permute-start | bytes 4616 | tf_op jit(solution)/shard_map/ppermute | solution.py:36
  10.0 17.5 %collective-permute-start = (bf16[3,768]{1,0:T(4,128)(2,1)S(1)}, bf16[3,768]{1,0:T(4,128)(2,1)S(1)}, u32[]{:S(2)}, u32[]{:S(2)}) collective-permute-start(bf16[3,768]{1,0:T(4,128)(2,1)S(1)} %slice.72), channel_id=1, source_target_pairs={{0,8},{8,16},{16,24},{24,32},{32,40},{40,48},{48,56},{56,64},{64,7... | collective-permute-start | bytes 13832 | tf_op jit(solution)/shard_map/ppermute | solution.py:36
  27.5 11.1 %copy-start.2 = (f32[12]{0:T(128)S(1)}, f32[12]{0:T(128)}, u32[]{:S(2)}) copy-start(f32[12]{0:T(128)} %param.20) | copy-start | bytes 148
  38.6 68.4 %copy-start.3 = (u32[256]{0:T(256)S(1)}, u32[256]{0:T(256)}, u32[]{:S(2)}) copy-start(u32[256]{0:T(256)} %constant.66) | copy-start | bytes 3076
  217.1 44.0 %copy-start.1 = (f32[768]{0:T(1024)S(1)}, f32[768]{0:T(1024)}, u32[]{:S(2)}) copy-start(f32[768]{0:T(1024)} %param.21) | copy-start | bytes 9220
Sparse Core Ops, SparseCore 0:
  107.0 56.1 all-gather.3
where the time goes:
time: 275 us; the launch traced here: 273 us
  blocking collectives  91.7 us (33%)
  other arithmetic  82.1 us (30%)
  local copies, waits for them, and re-layouts  53.5 us (19%)
  matrix products  26.3 us (10%)
  between operations  14.2 us (5%)
  starting transfers between devices  3.82 us (1%)
    unnamed x1, blocking collectives  58.9 us
    psum x1, blocking collectives, mamba_layer(): square_sum = lax.psum(jnp.sum(gated_rows * gated_rows, axis=1), 'head')  32.8 us
    add x30, other arithmetic, combine(): jnp.exp(later[0])[:, None, None] * earlier[1] + later[1]  32 us
    convert_element_type x2, other arithmetic, conv_silu(): return jax.nn.silu(running).astype(jnp.bfloat16)  13.7 us
    dynamic_slice x40, local copies, waits for them, and re-layouts, mamba_layer(): lax.scan(advance, start_state, (xs_rows.reshape(block_count, BLOCK, width...  13.2 us
    dynamic_update_slice x20, local copies, waits for them, and re-layouts, mamba_layer(): lax.scan(advance, start_state, (xs_rows.reshape(block_count, BLOCK, width...  12.1 us
    reduce_sum x1, other arithmetic, mamba_layer(): square_sum = lax.psum(jnp.sum(gated_rows * gated_rows, axis=1), 'head')  11.1 us
    dot_general x10, matrix products, advance(): jnp.einsum('hij,jhp->ihp', weights, xs_heads, preferred_element_type=jnp....  10.3 us
  transfers between devices with their start and end apart: 3, of which 0 were waited for; matrix products, arithmetic and copies ran while one was open for 7% of the time, Pallas kernels for 0%

commit v1 on v0

v1 whole, which is shorter than its diff:
```python
import functools

import jax
import jax.numpy as jnp
from jax import lax
from jax.experimental import pallas as pl
from jax.experimental.pallas import tpu as pltpu
from jax.sharding import PartitionSpec as P

HP = 64
NS = 128
CONV = 4
Q = 128
HALO = 16
PIECES = 32
LOG2E = 1.4426950408889634
F32 = jnp.float32
BF16 = jnp.bfloat16
MESH = pl.DeviceIdType.MESH


def dot(a, b, ca=1, cb=0, precision=None):
    return lax.dot_general(
        a, b, (((ca,), (cb,)), ((), ())), preferred_element_type=F32, precision=precision
    )


def conv_half_silu(window, taps):
    h = None
    for o in range(CONV):
        start = HALO - (CONV - 1) + o
        term = window[start : start + Q] * taps[o : o + 1]
        h = term if h is None else h + term
    return h + h * jnp.tanh(h)


def kernel(
    nseq,
    nhead,
    x_hbm,
    bc_hbm,
    gate_hbm,
    ld_ref,
    dt_ref,
    kx_ref,
    kbc_ref,
    skip_ref,
    gain_ref,
    out_ref,
    xbuf,
    bcbuf,
    gbuf,
    ld16,
    dt16,
    xs_ref,
    bcs_ref,
    y_ref,
    u_ref,
    brow_ref,
    acol_ref,
    colb_ref,
    drow_ref,
    ohe_ref,
    oht_ref,
    oh16_ref,
    tri_ref,
    st_ref,
    dec_all,
    send1,
    recv1,
    send2,
    recv2,
    ss_all,
    in_sem,
    halo_send,
    halo_recv,
    dec_send,
    dec_recv,
    one_send,
    one_recv,
    two_send,
    two_recv,
    ss_send,
    ss_recv,
):
    heads = ld_ref.shape[0]
    rows, width = out_ref.shape
    nc = rows // Q
    half = width // 2
    per = PIECES // nseq
    lanes = width // 128
    groups = ss_send.shape[1]
    gsize = nc // groups
    inner = width * nhead
    me = lax.axis_index("seq")
    mz = lax.axis_index("head")

    def seq_peer(i):
        return lax.rem(me + i, nseq)

    def head_peer(i):
        return lax.rem(mz + i, nhead)

    def in_copies(c):
        at = pl.ds(pl.multiple_of(c * Q, Q), Q)
        to = pl.ds(pl.multiple_of(c * Q + HALO, HALO), Q)
        return (
            pltpu.make_async_copy(x_hbm.at[at], xbuf.at[to], in_sem.at[0, c]),
            pltpu.make_async_copy(bc_hbm.at[at], bcbuf.at[to], in_sem.at[1, c]),
            pltpu.make_async_copy(gate_hbm.at[at], gbuf.at[at], in_sem.at[2, c]),
        )

    def issue_in(i, _):
        c = nc - 1 - i
        copies = in_copies(c)
        copies[0].start()
        copies[1].start()
        return 0

    lax.fori_loop(0, nc, issue_in, 0)

    barrier = pltpu.get_barrier_semaphore()

    def greet_seq(i, _):
        pl.semaphore_signal(barrier, inc=1, device_id={"seq": seq_peer(i)}, device_id_type=MESH)
        return 0

    def greet_head(i, _):
        pl.semaphore_signal(barrier, inc=1, device_id={"head": head_peer(i)}, device_id_type=MESH)
        return 0

    lax.fori_loop(1, nseq, greet_seq, 0)
    lax.fori_loop(1, nhead, greet_head, 0)

    def issue_gate(i, _):
        in_copies(i)[2].start()
        return 0

    lax.fori_loop(0, nc, issue_gate, 0)

    def onehot(shape, picks):
        r = lax.broadcasted_iota(jnp.int32, shape, 0)
        h = lax.broadcasted_iota(jnp.int32, shape, 1) // HP
        hit = r == h + picks[0]
        for p in picks[1:]:
            hit = hit | (r == h + p)
        return jnp.where(hit, 1.0, 0.0)

    ohe_ref[...] = onehot((128, width), (16, 80)).astype(BF16)
    oht_ref[...] = onehot((128, width), (32, 96)).astype(BF16)
    oh16_ref[...] = onehot((16, width), (0,))
    row = lax.broadcasted_iota(jnp.int32, (Q, Q), 0)
    col = lax.broadcasted_iota(jnp.int32, (Q, Q), 1)
    tri_ref[...] = jnp.where(row <= col, 1.0, 0.0)
    ld16[...] = jnp.zeros_like(ld16)
    dt16[...] = jnp.ones_like(dt16)
    ld16[0:heads, :] = ld_ref[...]
    dt16[0:heads, :] = dt_ref[...]

    def spread(column):
        return jnp.sum(oh16_ref[...] * column, axis=0, keepdims=True)

    total = jnp.sum(ld16[...], axis=1, keepdims=True)
    dec_all[me] = spread(jnp.exp(total))
    st_ref[...] = jnp.zeros_like(st_ref)

    def halo_copies():
        peer = {"seq": seq_peer(1)}
        tail = pl.ds(rows, HALO)
        return (
            pltpu.make_async_remote_copy(
                xbuf.at[tail], xbuf.at[pl.ds(0, HALO)], halo_send.at[0], halo_recv.at[0],
                device_id=peer, device_id_type=MESH,
            ),
            pltpu.make_async_remote_copy(
                bcbuf.at[tail], bcbuf.at[pl.ds(0, HALO)], halo_send.at[1], halo_recv.at[1],
                device_id=peer, device_id_type=MESH,
            ),
        )

    def dec_copy(peer, source):
        return pltpu.make_async_remote_copy(
            dec_all.at[source], dec_all.at[source], dec_send.at[peer], dec_recv.at[source],
            device_id={"seq": peer}, device_id_type=MESH,
        )

    def phase_a(i, g):
        c = nc - 1 - i

        @pl.when(i == nc // 2)
        def _():
            pl.semaphore_wait(barrier, nseq - 1 + nhead - 1)
            for copy in halo_copies():
                copy.start()

            def send(k, _):
                dec_copy(seq_peer(k), me).start()
                return 0

            lax.fori_loop(1, nseq, send, 0)

        @pl.when(i < nc - 1)
        def _():
            copies = in_copies(c - 1)
            copies[0].wait()
            copies[1].wait()

        @pl.when(i == nc - 1)
        def _():
            for copy in halo_copies():
                copy.wait_recv()

            @pl.when(me == 0)
            def _():
                xbuf[0:HALO, :] = jnp.zeros((HALO, width), BF16)
                bcbuf[0:HALO, :] = jnp.zeros((HALO, 2 * NS), BF16)

        at = pl.ds(pl.multiple_of(c * Q, Q), Q)
        window = pl.ds(pl.multiple_of(c * Q, Q), Q + HALO)
        step = dt16[:, at]
        cum = dot(ld16[:, at], tri_ref[...], precision=lax.Precision.HIGHEST)
        tot = cum[:, Q - 1 : Q]
        brow_ref[c] = (cum - jnp.log(step)) * LOG2E
        from_start = jnp.exp(cum)
        to_end = jnp.exp(tot - cum) * step
        start_hi = from_start.astype(BF16).astype(F32)
        end_hi = to_end.astype(BF16).astype(F32)
        zero = jnp.zeros((16, Q), F32)
        stack = jnp.concatenate(
            [cum * LOG2E, start_hi, end_hi, zero, zero, from_start - start_hi, to_end - end_hi, zero],
            axis=0,
        ).T
        acol_ref[c] = stack
        stack = stack.astype(BF16)
        colb_ref[c] = stack
        drow_ref[c] = spread(jnp.exp(tot))
        grow = spread(jnp.exp(g))
        taps = kbc_ref[...].astype(F32) * 0.5
        bcs = [
            conv_half_silu(
                bcbuf[window, 128 * j : 128 * j + 128].astype(F32), taps[:, 128 * j : 128 * j + 128]
            ).astype(BF16)
            for j in range(2)
        ]
        bcs_ref[c, :, 0:128] = bcs[0]
        bcs_ref[c, :, 128:256] = bcs[1]
        taps = kx_ref[...].astype(F32) * 0.5
        for j in range(lanes):
            cols = slice(128 * j, 128 * j + 128)
            xs = conv_half_silu(xbuf[window, cols].astype(F32), taps[:, cols])
            xs_ref[c, :, cols] = xs.astype(BF16)
            weighted = (xs * dot(stack, oht_ref[:, cols])).astype(BF16)
            update = dot(bcs[0], weighted, 0, 0)
            u_ref[c, :, cols] = update
            st_ref[:, cols] += grow[:, cols] * update
        return g + tot

    copies = in_copies(nc - 1)
    copies[0].wait()
    copies[1].wait()
    lax.fori_loop(0, nc, phase_a, jnp.zeros((16, 1), F32))

    for q in range(PIECES):
        r, l = q // 2, q % 2
        send1[q // per, q % per] = st_ref[8 * r : 8 * r + 8, half * l : half * l + half].astype(BF16)
    recv1[me] = send1[me]

    def one_copy(peer, source):
        return pltpu.make_async_remote_copy(
            send1.at[peer], recv1.at[source], one_send.at[peer], one_recv.at[source],
            device_id={"seq": peer}, device_id_type=MESH,
        )

    def two_copy(peer, source):
        return pltpu.make_async_remote_copy(
            send2.at[peer], recv2.at[source], two_send.at[peer], two_recv.at[source],
            device_id={"seq": peer}, device_id_type=MESH,
        )

    def send_one(k, _):
        one_copy(seq_peer(k), me).start()
        return 0

    lax.fori_loop(1, nseq, send_one, 0)

    def second_round():
        def arrived(k, _):
            peer = seq_peer(k)
            dec_copy(peer, peer).wait_recv()
            one_copy(peer, peer).wait_recv()
            return 0

        lax.fori_loop(1, nseq, arrived, 0)
        for e in range(per):
            l = lax.rem(me * per + e, 2)
            cols = pl.ds(pl.multiple_of(l * half, 128), half)

            def scan(k, acc):
                send2[k, e] = acc.astype(BF16)
                return dec_all[k, :, cols] * acc + recv1[k, e].astype(F32)

            lax.fori_loop(0, nseq, scan, jnp.zeros((8, half), F32))
        recv2[me] = send2[me]

        def send_two(k, _):
            two_copy(seq_peer(k), me).start()
            return 0

        lax.fori_loop(1, nseq, send_two, 0)

    lane = lax.broadcasted_iota(jnp.int32, (Q, 128), 1)
    lower = lax.broadcasted_iota(jnp.int32, (Q, Q), 0) >= lax.broadcasted_iota(jnp.int32, (Q, Q), 1)

    def phase_b(c, _):
        @pl.when(c == nc // 2)
        def _():
            second_round()

        scores = jnp.where(lower, dot(bcs_ref[c, :, 128:256], bcs_ref[c, :, 0:128], 1, 1), 0.0)
        for j in range(lanes):
            cols = slice(128 * j, 128 * j + 128)
            weights = []
            for h in (2 * j, 2 * j + 1):
                gap = acol_ref[c, :, h : h + 1] - brow_ref[c, h : h + 1, :]
                weights.append((scores * jnp.exp2(jnp.minimum(gap, 0.0))).astype(BF16))
            xs = xs_ref[c, :, cols]
            pair = jnp.concatenate(
                [jnp.where(lane < HP, xs, 0.0).astype(BF16), jnp.where(lane < HP, 0.0, xs).astype(BF16)],
                axis=0,
            )
            intra = dot(jnp.concatenate(weights, axis=1), pair)
            skip = jnp.where(lane < HP, skip_ref[2 * j], skip_ref[2 * j + 1])
            y_ref[c, :, cols] = intra + skip * xs.astype(F32)
        return 0

    lax.fori_loop(0, nc, phase_b, 0)

    def arrived_two(k, _):
        peer = seq_peer(k)
        two_copy(peer, peer).wait_recv()
        return 0

    lax.fori_loop(1, nseq, arrived_two, 0)
    for q in range(PIECES):
        r, l = q // 2, q % 2
        st_ref[8 * r : 8 * r + 8, half * l : half * l + half] = recv2[q // per, q % per].astype(F32)

    def ss_copy(peer, source, g):
        part = pl.ds(g * gsize, gsize)
        return pltpu.make_async_remote_copy(
            ss_all.at[source, part], ss_all.at[source, part],
            ss_send.at[peer, g], ss_recv.at[source, g],
            device_id={"head": peer}, device_id_type=MESH,
        )

    def phase_c(c, _):
        in_copies(c)[2].wait()
        at = pl.ds(pl.multiple_of(c * Q, Q), Q)
        ss = None
        for j in range(lanes):
            cols = slice(128 * j, 128 * j + 128)
            state = st_ref[:, cols]
            carried = dot(bcs_ref[c, :, 128:256], state.astype(BF16))
            st_ref[:, cols] = drow_ref[c, :, cols] * state + u_ref[c, :, cols]
            mixed = y_ref[c, :, cols] + carried * dot(colb_ref[c], ohe_ref[:, cols])
            h = gbuf[at, cols].astype(F32) * 0.5
            gated = mixed * (h + h * jnp.tanh(h))
            y_ref[c, :, cols] = gated
            part = dot(jnp.ones((8, 128), BF16), (gated * gated).astype(BF16), 1, 1)
            ss = part if ss is None else ss + part
        ss_all[mz, c] = ss[0:1]
        return 0

    for g in range(groups):
        lax.fori_loop(g * gsize, (g + 1) * gsize, phase_c, 0)

        def send_ss(k, _):
            ss_copy(head_peer(k), mz, g).start()
            return 0

        lax.fori_loop(1, nhead, send_ss, 0)

    eye = lax.broadcasted_iota(jnp.int32, (Q, Q), 0) == lax.broadcasted_iota(jnp.int32, (Q, Q), 1)

    def phase_d(c, _):
        square = ss_all[0, c]
        for p in range(1, nhead):
            square = square + ss_all[p, c]
        scale = lax.rsqrt(square * (1.0 / inner) + 1e-05)
        scale = jnp.sum(jnp.where(eye, scale, 0.0), axis=1, keepdims=True)
        at = pl.ds(pl.multiple_of(c * Q, Q), Q)
        for j in range(lanes):
            cols = slice(128 * j, 128 * j + 128)
            out_ref[at, cols] = (y_ref[c, :, cols] * scale * gain_ref[:, cols]).astype(BF16)
        return 0

    for g in range(groups):

        def arrived_ss(k, _):
            peer = head_peer(k)
            ss_copy(peer, peer, g).wait_recv()
            return 0

        lax.fori_loop(1, nhead, arrived_ss, 0)
        lax.fori_loop(g * gsize, (g + 1) * gsize, phase_d, 0)

    for copy in halo_copies():
        copy.wait_send()

    def left_seq(k, _):
        peer = seq_peer(k)
        dec_copy(peer, me).wait_send()
        one_copy(peer, me).wait_send()
        two_copy(peer, me).wait_send()
        return 0

    lax.fori_loop(1, nseq, left_seq, 0)

    def left_head(k, _):
        for g in range(groups):
            ss_copy(head_peer(k), mz, g).wait_send()
        return 0

    lax.fori_loop(1, nhead, left_head, 0)


def per_device(nseq, nhead, x_in, bc_in, gate_in, log_decay, step_size, conv_x, conv_bc, skip_gain, norm_gain):
    rows, width = x_in.shape
    nc = rows // Q
    per = PIECES // nseq
    half = width // 2
    groups = 2
    vmem = pl.BlockSpec(memory_space=pltpu.VMEM)
    anywhere = pl.BlockSpec(memory_space=pl.ANY)
    dma = pltpu.SemaphoreType.DMA
    return pl.pallas_call(
        functools.partial(kernel, nseq, nhead),
        out_shape=jax.ShapeDtypeStruct((rows, width), BF16),
        in_specs=[
            anywhere, anywhere, anywhere, vmem, vmem, vmem, vmem,
            pl.BlockSpec(memory_space=pltpu.SMEM), vmem,
        ],
        out_specs=vmem,
        scratch_shapes=[
            pltpu.VMEM((HALO + rows, width), BF16),
            pltpu.VMEM((HALO + rows, 2 * NS), BF16),
            pltpu.VMEM((rows, width), BF16),
            pltpu.VMEM((16, rows), F32),
            pltpu.VMEM((16, rows), F32),
            pltpu.VMEM((nc, Q, width), BF16),
            pltpu.VMEM((nc, Q, 2 * NS), BF16),
            pltpu.VMEM((nc, Q, width), F32),
            pltpu.VMEM((nc, NS, width), F32),
            pltpu.VMEM((nc, 16, Q), F32),
            pltpu.VMEM((nc, Q, 128), F32),
            pltpu.VMEM((nc, Q, 128), BF16),
            pltpu.VMEM((nc, 1, width), F32),
            pltpu.VMEM((128, width), BF16),
            pltpu.VMEM((128, width), BF16),
            pltpu.VMEM((16, width), F32),
            pltpu.VMEM((Q, Q), F32),
            pltpu.VMEM((NS, width), F32),
            pltpu.VMEM((nseq, 1, width), F32),
            pltpu.VMEM((nseq, per, 8, half), BF16),
            pltpu.VMEM((nseq, per, 8, half), BF16),
            pltpu.VMEM((nseq, per, 8, half), BF16),
            pltpu.VMEM((nseq, per, 8, half), BF16),
            pltpu.VMEM((nhead, nc, 1, Q), F32),
            dma((3, nc)),
            dma((2,)), dma((2,)),
            dma((nseq,)), dma((nseq,)),
            dma((nseq,)), dma((nseq,)),
            dma((nseq,)), dma((nseq,)),
            dma((nhead, groups)), dma((nhead, groups)),
        ],
        compiler_params=pltpu.CompilerParams(
            collective_id=0, has_side_effects=True, vmem_limit_bytes=60 * 1024 * 1024
        ),
        name="mamba",
    )(
        x_in, bc_in, gate_in, log_decay, step_size, conv_x, conv_bc, skip_gain,
        norm_gain.reshape(1, width),
    )


def solution(mesh):
    in_specs = (
        P("seq", "head"),
        P("seq", None),
        P("seq", "head"),
        P("head", "seq"),
        P("head", "seq"),
        P(None, "head"),
        P(),
        P("head"),
        P("head"),
    )
    return jax.shard_map(
        functools.partial(per_device, mesh.shape["seq"], mesh.shape["head"]),
        mesh=mesh,
        in_specs=in_specs,
        out_specs=P("seq", "head"),
        check_vma=False,
    )
```

time: 275 us -> 70.2 us (0.26)
  the two profiles are of different devices: /device:TPU:30 before, /device:TPU:1 now
where the time goes in v1:
time: 70.2 us; the launch traced here: 70.1 us
  Pallas kernels  64.5 us (92%)
  local copies, waits for them, and re-layouts  5.56 us (8%)
    pallas_call x1, Pallas kernels, per_device(): pl.pallas_call(functools.partial(kernel, nseq, nhead), out_shape=jax.Shap...  64.5 us
    unnamed x1, local copies, waits for them, and re-layouts  4.29 us

profile of v1, /device:TPU:1, one launch (start us, length us, event | category | flops | bytes accessed | tf_op | source)
XLA Modules:
  0.0 70.1 jit_solution(6738359264205995108)
XLA Ops:
  0.0 1.3 %reshape.3.gain_ref = f32[1,768]{1,0:T(1,128)} reshape(f32[768]{0:T(1024)} %param.17) | data formatting | bytes 6144 | tf_op jit(solution)/shard_map/reshape | solution.py:482
  1.3 64.5 %mamba.1 = bf16[2560,768]{1,0:T(8,128)(2,1)} custom-call(bf16[2560,768]{1,0:T(8,128)(2,1)} %x_hbm.1, bf16[2560,256]{1,0:T(8,128)(2,1)} %bc_hbm.1, bf16[2560,768]{1,0:T(8,128)(2,1)} %gate_hbm.1, f32[12,2560]{1,0:T(8,128)} %ld_ref.1, f32[12,2560]{1,0:T(8,128)} %dt_ref.1, bf16[4,768]{1,0:T(4,128)(2,1)} %kx_ref.1, bf16[4,256]{1,0:T(4,128)(2,1)} %kbc_ref.1, ...), custom_call_target="tpu_custom_call" | custom-call | tf_op jit(solution)/shard_map/mamba/pallas_call | solution.py:436
  65.8 4.3 %copy.11 = bf16[2560,768]{1,0:T(8,128)(2,1)} copy(bf16[2560,768]{1,0:T(8,128)(2,1)} %mamba.1) | data formatting | bytes 7864320

commit v2 on v1

v2 whole, which is shorter than its diff:
```python
import functools

import jax
import jax.numpy as jnp
from jax import lax
from jax.experimental import pallas as pl
from jax.experimental.pallas import tpu as pltpu
from jax.sharding import PartitionSpec as P

HP = 64
NS = 128
CONV = 4
Q = 128
HALO = 16
PIECES = 32
IN_PIECES = 5
GREET_PIECE = 2
UNROLL_B = 1
VMEM_LIMIT = 56 * 1024 * 1024
LOG2E = 1.4426950408889634
F32 = jnp.float32
BF16 = jnp.bfloat16
MESH = pl.DeviceIdType.MESH


def dot(a, b, ca=1, cb=0, precision=None):
    return lax.dot_general(
        a, b, (((ca,), (cb,)), ((), ())), preferred_element_type=F32, precision=precision
    )


def conv_half_silu(window, taps, shift):
    shift[...] = window[HALO - 8 :].astype(F32)
    h = None
    for o in range(CONV):
        start = 8 - (CONV - 1) + o
        term = shift[start : start + Q] * taps[o : o + 1]
        h = term if h is None else h + term
    return h + h * jnp.tanh(h)


def kernel(
    nseq,
    nhead,
    x_hbm,
    bc_hbm,
    gate_hbm,
    ld_hbm,
    dt_hbm,
    kx_hbm,
    kbc_hbm,
    skip_hbm,
    gain_hbm,
    out_ref,
    ld_ref,
    dt_ref,
    kx_ref,
    kbc_ref,
    skip_ref,
    xbuf,
    bcbuf,
    gbuf,
    ldc,
    dtc,
    start_ref,
    tot_ref,
    xs_ref,
    bcs_ref,
    y_ref,
    gain_ref,
    u_ref,
    brow_ref,
    acol_ref,
    sg_ref,
    colb_ref,
    drow_ref,
    grow_ref,
    ohe_ref,
    oht_ref,
    ohw_ref,
    tri_ref,
    st_ref,
    shift_ref,
    into_ref,
    intob_ref,
    dec_all,
    send1,
    recv1,
    send2,
    recv2,
    ss_all,
    in_sem,
    small_sem,
    halo_send,
    halo_recv,
    dec_send,
    dec_recv,
    one_send,
    one_recv,
    two_send,
    two_recv,
    ss_send,
    ss_recv,
):
    heads = ld_ref.shape[0]
    rows, width = out_ref.shape
    nc = rows // Q
    half = width // 2
    per = PIECES // nseq
    lanes = width // 128
    groups = ((0, nc - nc // 5), (nc - nc // 5, nc))
    inner = width * nhead
    me = lax.axis_index("seq")
    mz = lax.axis_index("head")

    def seq_peer(i):
        return lax.rem(me + i, nseq)

    def head_peer(i):
        return lax.rem(mz + i, nhead)

    piece = rows // IN_PIECES
    blocks = nc // IN_PIECES

    def in_copies(k):
        at = pl.ds(pl.multiple_of(k * piece, piece), piece)
        to = pl.ds(pl.multiple_of(k * piece + HALO, HALO), piece)
        return (
            pltpu.make_async_copy(x_hbm.at[at], xbuf.at[to], in_sem.at[0, k]),
            pltpu.make_async_copy(bc_hbm.at[at], bcbuf.at[to], in_sem.at[1, k]),
        )

    gate_copy = pltpu.make_async_copy(gate_hbm, gbuf, in_sem.at[2, 0])

    small = [
        pltpu.make_async_copy(source, target, small_sem.at[k])
        for k, (source, target) in enumerate(
            [(ld_hbm, ld_ref), (dt_hbm, dt_ref), (kx_hbm, kx_ref), (kbc_hbm, kbc_ref), (skip_hbm, skip_ref), (gain_hbm, gain_ref)]
        )
    ]
    for copy in small:
        copy.start()
    for k in reversed(range(IN_PIECES)):
        for copy in in_copies(k):
            copy.start()

    barrier = pltpu.get_barrier_semaphore()

    def greet_seq(i, _):
        pl.semaphore_signal(barrier, inc=1, device_id={"seq": seq_peer(i)}, device_id_type=MESH)
        return 0

    def greet_head(i, _):
        pl.semaphore_signal(barrier, inc=1, device_id={"head": head_peer(i)}, device_id_type=MESH)
        return 0

    lax.fori_loop(1, nseq, greet_seq, 0)
    lax.fori_loop(1, nhead, greet_head, 0)

    gate_copy.start()

    def onehot(shape, picks):
        r = lax.broadcasted_iota(jnp.int32, shape, 0)
        h = lax.broadcasted_iota(jnp.int32, shape, 1) // HP
        hit = r == h + picks[0]
        for p in picks[1:]:
            hit = hit | (r == h + p)
        return jnp.where(hit, 1.0, 0.0)

    ohe_ref[...] = onehot((128, width), (16, 80)).astype(BF16)
    oht_ref[...] = onehot((128, width), (32, 96)).astype(BF16)
    ohw_ref[...] = onehot((128, width), (48, 64)).astype(BF16)
    row = lax.broadcasted_iota(jnp.int32, (Q, Q), 0)
    col = lax.broadcasted_iota(jnp.int32, (Q, Q), 1)
    tri_ref[...] = jnp.where(row <= col, 1.0, 0.0)
    tops = lax.broadcasted_iota(jnp.int32, (24, 24), 0)
    rests = lax.broadcasted_iota(jnp.int32, (24, 24), 1)
    later = jnp.where((rests > tops) & (rests < nc), 1.0, 0.0)
    ldc[...] = jnp.zeros_like(ldc)
    dtc[...] = jnp.ones_like(dtc)
    tot_ref[...] = jnp.zeros_like(tot_ref)
    for copy in small:
        copy.wait()
    for c in range(nc):
        at = slice(c * Q, c * Q + Q)
        ldc[16 * c : 16 * c + heads, :] = ld_ref[:, at]
        dtc[16 * c : 16 * c + heads, :] = dt_ref[:, at]

    cum = dot(ldc[...], tri_ref[...], precision=lax.Precision.HIGHEST)
    step = dtc[...]
    tot = cum[:, Q - 1 : Q]
    brow_ref[...] = (cum - jnp.log(step)) * LOG2E
    ldc[...] = cum * LOG2E
    from_start = jnp.exp(cum)
    to_end = jnp.exp(tot - cum) * step
    start_ref[...] = from_start
    dtc[...] = to_end

    def turn(c, base):
        at = pl.ds(pl.multiple_of(16 * c, 16), 16)
        first, last = start_ref[at, :], dtc[at, :]
        first_hi = first.astype(BF16).astype(F32)
        last_hi = last.astype(BF16).astype(F32)
        power = ldc[at, :]
        whole = jnp.exp2(power + base)
        whole_hi = whole.astype(BF16).astype(F32)
        stack = jnp.concatenate(
            [
                power, first_hi, last_hi, whole_hi, whole - whole_hi, first - first_hi, last - last_hi,
                jnp.zeros((16, Q), F32),
            ],
            axis=0,
        ).T
        acol_ref[c] = stack
        colb_ref[c] = stack.astype(BF16)
        tot_ref[pl.ds(c, 1), :] = stack[Q - 1 : Q, :]
        return base + power[:, Q - 1 : Q]

    lax.fori_loop(0, nc, turn, jnp.zeros((16, 1), F32), unroll=5)

    heads_only = lax.broadcasted_iota(jnp.int32, (24, 128), 1) < 16
    totals = jnp.where(heads_only, tot_ref[...], 0.0)
    ohf = onehot((128, width), (0,))

    def expand(powers):
        return dot(jnp.exp2(powers), ohf, precision=lax.Precision.HIGHEST)

    drow_ref[...] = expand(totals)
    grow_ref[...] = expand(dot(later, totals, precision=lax.Precision.HIGHEST))
    dec_all[me] = expand(jnp.sum(totals, axis=0, keepdims=True) + jnp.zeros((8, 128), F32))[0:1]
    st_ref[...] = jnp.zeros_like(st_ref)

    def halo_copies():
        peer = {"seq": seq_peer(1)}
        tail = pl.ds(rows, HALO)
        return (
            pltpu.make_async_remote_copy(
                xbuf.at[tail], xbuf.at[pl.ds(0, HALO)], halo_send.at[0], halo_recv.at[0],
                device_id=peer, device_id_type=MESH,
            ),
            pltpu.make_async_remote_copy(
                bcbuf.at[tail], bcbuf.at[pl.ds(0, HALO)], halo_send.at[1], halo_recv.at[1],
                device_id=peer, device_id_type=MESH,
            ),
        )

    def dec_copy(peer, source):
        return pltpu.make_async_remote_copy(
            dec_all.at[source], dec_all.at[source], dec_send.at[peer], dec_recv.at[source],
            device_id={"seq": peer}, device_id_type=MESH,
        )

    def phase_a(c, side):
        window = pl.ds(pl.multiple_of(c * Q, Q), Q + HALO)
        stack = colb_ref[c]
        grow = grow_ref[pl.ds(c, 1), :]
        taps = kbc_ref[...].astype(F32) * 0.5
        bcs = [
            conv_half_silu(
                bcbuf[window, 128 * j : 128 * j + 128], taps[:, 128 * j : 128 * j + 128],
                shift_ref.at[side, lanes + j],
            ).astype(BF16)
            for j in range(2)
        ]
        bcs_ref[c, :, 0:128] = bcs[0]
        bcs_ref[c, :, 128:256] = bcs[1]
        taps = kx_ref[...].astype(F32) * 0.5
        for j in range(0, lanes, 2):
            wide = slice(128 * j, 128 * j + 256)
            ends = dot(stack, oht_ref[:, wide])
            weighted = []
            for t in range(2):
                cols = slice(128 * (j + t), 128 * (j + t) + 128)
                xs = conv_half_silu(xbuf[window, cols], taps[:, cols], shift_ref.at[side, j + t])
                xs_ref[c, :, cols] = xs.astype(BF16)
                weighted.append((xs * ends[:, 128 * t : 128 * t + 128]).astype(BF16))
            update = dot(bcs[0], jnp.concatenate(weighted, axis=1), 0, 0)
            u_ref[c, :, wide] = update
            st_ref[:, wide] += grow[:, wide] * update

    def piece_a(i, _):
        k = IN_PIECES - 1 - i

        @pl.when(k > 0)
        def _():
            for copy in in_copies(k - 1):
                copy.wait()

        @pl.when(i == GREET_PIECE)
        def _():
            pl.semaphore_wait(barrier, nseq - 1 + nhead - 1)
            for copy in halo_copies():
                copy.start()

            def send(k, _):
                dec_copy(seq_peer(k), me).start()
                return 0

            lax.fori_loop(1, nseq, send, 0)

        @pl.when(k == 0)
        def _():
            for copy in halo_copies():
                copy.wait_recv()

            @pl.when(me == 0)
            def _():
                xbuf[0:HALO, :] = jnp.zeros((HALO, width), BF16)
                bcbuf[0:HALO, :] = jnp.zeros((HALO, 2 * NS), BF16)

        def block(b, _):
            for side in range(2):
                phase_a(k * blocks + blocks - 1 - 2 * b - side, side)
            return 0

        lax.fori_loop(0, blocks // 2, block, 0)
        return 0

    for copy in in_copies(IN_PIECES - 1):
        copy.wait()
    lax.fori_loop(0, IN_PIECES, piece_a, 0)

    for q in range(PIECES):
        r, l = q // 2, q % 2
        send1[q // per, q % per] = st_ref[8 * r : 8 * r + 8, half * l : half * l + half].astype(BF16)
    recv1[me] = send1[me]

    def one_copy(peer, source):
        return pltpu.make_async_remote_copy(
            send1.at[peer], recv1.at[source], one_send.at[peer], one_recv.at[source],
            device_id={"seq": peer}, device_id_type=MESH,
        )

    def two_copy(peer, source):
        return pltpu.make_async_remote_copy(
            send2.at[peer], recv2.at[source], two_send.at[peer], two_recv.at[source],
            device_id={"seq": peer}, device_id_type=MESH,
        )

    def send_one(k, _):
        one_copy(seq_peer(k), me).start()
        return 0

    lax.fori_loop(1, nseq, send_one, 0)

    def second_round():
        def arrived(k, _):
            peer = seq_peer(k)
            dec_copy(peer, peer).wait_recv()
            one_copy(peer, peer).wait_recv()
            return 0

        lax.fori_loop(1, nseq, arrived, 0)
        for e in range(per):
            l = lax.rem(me * per + e, 2)
            cols = pl.ds(pl.multiple_of(l * half, 128), half)

            def scan(k, acc):
                send2[k, e] = acc.astype(BF16)
                return dec_all[k, :, cols] * acc + recv1[k, e].astype(F32)

            lax.fori_loop(0, nseq, scan, jnp.zeros((8, half), F32))
        recv2[me] = send2[me]

        def send_two(k, _):
            two_copy(seq_peer(k), me).start()
            return 0

        lax.fori_loop(1, nseq, send_two, 0)

    lane = lax.broadcasted_iota(jnp.int32, (Q, 128), 1)
    left = jnp.where(lane < HP, 1.0, 0.0).astype(BF16)
    right = jnp.where(lane < HP, 0.0, 1.0).astype(BF16)
    lower = lax.broadcasted_iota(jnp.int32, (Q, Q), 0) >= lax.broadcasted_iota(jnp.int32, (Q, Q), 1)

    def phase_b(c, _):
        drow = drow_ref[pl.ds(c, 1), :]
        at = pl.ds(pl.multiple_of(c * Q, Q), Q)
        scores = jnp.where(lower, dot(bcs_ref[c, :, 128:256], bcs_ref[c, :, 0:128], 1, 1), 0.0)
        for j in range(lanes):
            cols = slice(128 * j, 128 * j + 128)
            weights = []
            for h in (2 * j, 2 * j + 1):
                gap = acol_ref[c, :, h : h + 1] - brow_ref[pl.ds(16 * c + h, 1), :]
                weights.append((scores * jnp.exp2(jnp.minimum(gap, 0.0))).astype(BF16))
            xs = xs_ref[c, :, cols]
            pair = jnp.concatenate([xs * left, xs * right], axis=0)
            intra = dot(jnp.concatenate(weights, axis=1), pair)
            skip = jnp.where(lane < HP, skip_ref[2 * j], skip_ref[2 * j + 1])
            state = st_ref[:, cols]
            st_ref[:, cols] = drow[:, cols] * state + u_ref[c, :, cols]
            if j % 2 == 0:
                wide = slice(128 * j, 128 * j + 256)
                decays = dot(colb_ref[c], ohe_ref[:, wide])
                before = []
            before.append(state.astype(BF16))
            y = intra + skip * xs.astype(F32)
            if j % 2 == 1:
                carried = dot(bcs_ref[c, :, 128:256], jnp.concatenate(before, axis=1)) * decays
                y_ref[c, :, 128 * j - 128 : 128 * j] = held + carried[:, :128]
                y_ref[c, :, cols] = y + carried[:, 128:]
            held = y
            h = (gbuf[at, cols] * jnp.asarray(0.5, BF16)).astype(F32)
            sg_ref[c, :, cols] = h + h * jnp.tanh(h)
        return 0

    gate_copy.wait()
    st_ref[...] = jnp.zeros_like(st_ref)
    split = nc // 4 * 2
    lax.fori_loop(0, split, phase_b, 0, unroll=UNROLL_B)
    second_round()
    lax.fori_loop(split, nc, phase_b, 0, unroll=UNROLL_B)

    def arrived_two(k, _):
        peer = seq_peer(k)
        two_copy(peer, peer).wait_recv()
        return 0

    lax.fori_loop(1, nseq, arrived_two, 0)
    for q in range(PIECES):
        r, l = q // 2, q % 2
        into_ref[8 * r : 8 * r + 8, half * l : half * l + half] = recv2[q // per, q % per].astype(F32)
    intob_ref[...] = into_ref[...].astype(BF16)

    def ss_copy(peer, source, g):
        part = pl.ds(groups[g][0], groups[g][1] - groups[g][0])
        return pltpu.make_async_remote_copy(
            ss_all.at[source, part], ss_all.at[source, part],
            ss_send.at[peer, g], ss_recv.at[source, g],
            device_id={"head": peer}, device_id_type=MESH,
        )

    def phase_c(i, _):
        both = pl.ds(2 * i, 2)
        cs = bcs_ref[both, :, 128:256].reshape(2 * Q, 128)
        columns = colb_ref[both].reshape(2 * Q, 128)
        ss = None
        for j in range(0, lanes, 2):
            wide = slice(128 * j, 128 * j + 256)
            carried = dot(cs, intob_ref[:, wide]) * dot(columns, ohw_ref[:, wide])
            mixed = y_ref[both, :, wide].reshape(2 * Q, 256) + carried
            gated = mixed * sg_ref[both, :, wide].reshape(2 * Q, 256)
            u_ref[both, :, wide] = gated.reshape(2, Q, 256)
            square = gated * gated
            part = square[:, :128] + square[:, 128:]
            ss = part if ss is None else ss + part
        ss = ss.astype(BF16)
        for t in range(2):
            ss_all[mz, 2 * i + t] = dot(jnp.ones((8, 128), BF16), ss[Q * t : Q * t + Q], 1, 1)[0:1]
        return 0

    for g in range(len(groups)):
        lax.fori_loop(groups[g][0] // 2, groups[g][1] // 2, phase_c, 0)

        def send_ss(k, _):
            ss_copy(head_peer(k), mz, g).start()
            return 0

        lax.fori_loop(1, nhead, send_ss, 0)

    eye = lax.broadcasted_iota(jnp.int32, (Q, Q), 0) == lax.broadcasted_iota(jnp.int32, (Q, Q), 1)
    gain = gain_ref[...].reshape(1, width)

    def phase_d(c, _):
        square = ss_all[0, c]
        for p in range(1, nhead):
            square = square + ss_all[p, c]
        scale = lax.rsqrt(square * (1.0 / inner) + 1e-05)
        scale = jnp.sum(jnp.where(eye, scale, 0.0), axis=1, keepdims=True)
        at = pl.ds(pl.multiple_of(c * Q, Q), Q)
        for j in range(lanes):
            cols = slice(128 * j, 128 * j + 128)
            out_ref[at, cols] = (u_ref[c, :, cols] * scale * gain[:, cols]).astype(BF16)
        return 0

    for g in range(len(groups)):

        def arrived_ss(k, _):
            peer = head_peer(k)
            ss_copy(peer, peer, g).wait_recv()
            return 0

        lax.fori_loop(1, nhead, arrived_ss, 0)
        lax.fori_loop(*groups[g], phase_d, 0, unroll=2)

    for copy in halo_copies():
        copy.wait_send()

    def left_seq(k, _):
        peer = seq_peer(k)
        dec_copy(peer, me).wait_send()
        one_copy(peer, me).wait_send()
        two_copy(peer, me).wait_send()
        return 0

    lax.fori_loop(1, nseq, left_seq, 0)

    def left_head(k, _):
        for g in range(len(groups)):
            ss_copy(head_peer(k), mz, g).wait_send()
        return 0

    lax.fori_loop(1, nhead, left_head, 0)


def per_device(nseq, nhead, x_in, bc_in, gate_in, log_decay, step_size, conv_x, conv_bc, skip_gain, norm_gain):
    rows, width = x_in.shape
    heads = log_decay.shape[0]
    nc = rows // Q
    per = PIECES // nseq
    half = width // 2
    groups = 2
    vmem = pl.BlockSpec(memory_space=pltpu.VMEM)
    dma = pltpu.SemaphoreType.DMA
    return pl.pallas_call(
        functools.partial(kernel, nseq, nhead),
        out_shape=pltpu.VMEM((rows, width), BF16),
        in_specs=[pl.BlockSpec(memory_space=pltpu.HBM)] * 9,
        out_specs=vmem,
        scratch_shapes=[
            pltpu.VMEM((heads, rows), F32),
            pltpu.VMEM((heads, rows), F32),
            pltpu.VMEM((CONV, width), BF16),
            pltpu.VMEM((CONV, 2 * NS), BF16),
            pltpu.SMEM((heads,), F32),
            pltpu.VMEM((HALO + rows, width), BF16),
            pltpu.VMEM((HALO + rows, 2 * NS), BF16),
            pltpu.VMEM((rows, width), BF16),
            pltpu.VMEM((16 * nc, Q), F32),
            pltpu.VMEM((16 * nc, Q), F32),
            pltpu.VMEM((16 * nc, Q), F32),
            pltpu.VMEM((24, 128), F32),
            pltpu.VMEM((nc, Q, width), BF16),
            pltpu.VMEM((nc, Q, 2 * NS), BF16),
            pltpu.VMEM((nc, Q, width), F32),
            pltpu.VMEM((width,), F32),
            pltpu.VMEM((nc, NS, width), F32),
            pltpu.VMEM((16 * nc, Q), F32),
            pltpu.VMEM((nc, Q, 128), F32),
            pltpu.VMEM((nc, Q, width), F32),
            pltpu.VMEM((nc, Q, 128), BF16),
            pltpu.VMEM((24, width), F32),
            pltpu.VMEM((24, width), F32),
            pltpu.VMEM((128, width), BF16),
            pltpu.VMEM((128, width), BF16),
            pltpu.VMEM((128, width), BF16),
            pltpu.VMEM((Q, Q), F32),
            pltpu.VMEM((NS, width), F32),
            pltpu.VMEM((2, width // 128 + 2, Q + 8, 128), F32),
            pltpu.VMEM((NS, width), F32),
            pltpu.VMEM((NS, width), BF16),
            pltpu.VMEM((nseq, 1, width), F32),
            pltpu.VMEM((nseq, per, 8, half), BF16),
            pltpu.VMEM((nseq, per, 8, half), BF16),
            pltpu.VMEM((nseq, per, 8, half), BF16),
            pltpu.VMEM((nseq, per, 8, half), BF16),
            pltpu.VMEM((nhead, nc, 1, Q), F32),
            dma((3, IN_PIECES)),
            dma((6,)),
            dma((2,)), dma((2,)),
            dma((nseq,)), dma((nseq,)),
            dma((nseq,)), dma((nseq,)),
            dma((nseq,)), dma((nseq,)),
            dma((nhead, groups)), dma((nhead, groups)),
        ],
        compiler_params=pltpu.CompilerParams(
            collective_id=0, has_side_effects=True, vmem_limit_bytes=VMEM_LIMIT
        ),
        name="mamba",
    )(
        *(
            pltpu.with_memory_space_constraint(a, pltpu.HBM)
            for a in (x_in, bc_in, gate_in, log_decay, step_size, conv_x, conv_bc, skip_gain, norm_gain)
        )
    )


def solution(mesh):
    in_specs = (
        P("seq", "head"),
        P("seq", None),
        P("seq", "head"),
        P("head", "seq"),
        P("head", "seq"),
        P(None, "head"),
        P(),
        P("head"),
        P("head"),
    )
    return jax.shard_map(
        functools.partial(per_device, mesh.shape["seq"], mesh.shape["head"]),
        mesh=mesh,
        in_specs=in_specs,
        out_specs=P("seq", "head"),
        check_vma=False,
    )
```

time: 70.2 us -> 48 us (0.68)
  Pallas kernels: 64.5 us -> 46 us
  local copies, waits for them, and re-layouts: 5.56 us -> 1.93 us
    pallas_call x1, Pallas kernels: 64.5 us -> 46 us  [per_device(): pl.pallas_call(functools.partial(kernel, nseq, nhead), out_shape=pltpu.VM...]
    unnamed x1, local copies, waits for them, and re-layouts: 4.29 us -> 1.93 us
    reshape x1 -> x0, local copies, waits for them, and re-layouts: 1.27 us -> none  [per_device(): norm_gain.reshape(1, width)]
where the time goes in v2:
time: 48 us
  Pallas kernels  46 us (96%)
  local copies, waits for them, and re-layouts  1.93 us (4%)
    pallas_call x1, Pallas kernels, per_device(): pl.pallas_call(functools.partial(kernel, nseq, nhead), out_shape=pltpu.VM...  46 us
    unnamed x1, local copies, waits for them, and re-layouts  1.93 us

profile of v2, /device:TPU:1, one launch (start us, length us, event | category | flops | bytes accessed | tf_op | source)
XLA Modules:
  0.0 48.0 jit_solution(3746168475380592365)
XLA Ops:
  0.0 46.0 %mamba.1 = bf16[2560,768]{1,0:T(8,128)(2,1)S(1)} custom-call(bf16[2560,768]{1,0:T(8,128)(2,1)} %x_hbm.1, bf16[2560,256]{1,0:T(8,128)(2,1)} %bc_hbm.1, bf16[2560,768]{1,0:T(8,128)(2,1)} %gate_hbm.1, f32[12,2560]{1,0:T(8,128)} %ld_hbm.1, f32[12,2560]{1,0:T(8,128)} %dt_hbm.1, bf16[4,768]{1,0:T(4,128)(2,1)} %kx_hbm.1, bf16[4,256]{1,0:T(4,128)(2,1)} %kbc_hbm.1, ...), custom_call_target="tpu_custom_call" | custom-call | tf_op jit(solution)/shard_map/mamba/pallas_call | solution.py:515
  46.0 1.9 %copy.11 = bf16[2560,768]{1,0:T(8,128)(2,1)} copy(bf16[2560,768]{1,0:T(8,128)(2,1)S(1)} %mamba.1) | data formatting | bytes 7864320

commit v3 on v2

--- a/solution.py
+++ b/solution.py
@@ -15,7 +15,6 @@
 PIECES = 32
 IN_PIECES = 5
 GREET_PIECE = 2
-UNROLL_B = 1
 VMEM_LIMIT = 56 * 1024 * 1024
 LOG2E = 1.4426950408889634
 F32 = jnp.float32
@@ -27,6 +26,13 @@
     return lax.dot_general(
         a, b, (((ca,), (cb,)), ((), ())), preferred_element_type=F32, precision=precision
     )
+
+
+def thirds(a):
+    hi = a.astype(BF16)
+    rest = a - hi.astype(F32)
+    mid = rest.astype(BF16)
+    return hi, mid, (rest - mid.astype(F32)).astype(BF16)
 
 
 def conv_half_silu(window, taps, shift):
@@ -108,7 +114,7 @@
     half = width // 2
     per = PIECES // nseq
     lanes = width // 128
-    groups = ((0, nc - nc // 5), (nc - nc // 5, nc))
+    groups = ((0, nc // 5 * 2), (nc // 5 * 2, nc // 5 * 4), (nc // 5 * 4, nc))
     inner = width * nhead
     me = lax.axis_index("seq")
     mz = lax.axis_index("head")
@@ -186,7 +192,8 @@
         ldc[16 * c : 16 * c + heads, :] = ld_ref[:, at]
         dtc[16 * c : 16 * c + heads, :] = dt_ref[:, at]
 
-    cum = dot(ldc[...], tri_ref[...], precision=lax.Precision.HIGHEST)
+    tri = tri_ref[...].astype(BF16)
+    cum = dot(jnp.concatenate(thirds(ldc[...]), axis=1), jnp.concatenate([tri, tri, tri], axis=0))
     step = dtc[...]
     tot = cum[:, Q - 1 : Q]
     brow_ref[...] = (cum - jnp.log(step)) * LOG2E
@@ -220,14 +227,21 @@
 
     heads_only = lax.broadcasted_iota(jnp.int32, (24, 128), 1) < 16
     totals = jnp.where(heads_only, tot_ref[...], 0.0)
-    ohf = onehot((128, width), (0,))
-
-    def expand(powers):
-        return dot(jnp.exp2(powers), ohf, precision=lax.Precision.HIGHEST)
-
-    drow_ref[...] = expand(totals)
-    grow_ref[...] = expand(dot(later, totals, precision=lax.Precision.HIGHEST))
-    dec_all[me] = expand(jnp.sum(totals, axis=0, keepdims=True) + jnp.zeros((8, 128), F32))[0:1]
+    exponents = jnp.concatenate(
+        [
+            totals,
+            dot(later, totals, precision=lax.Precision.HIGHEST),
+            jnp.sum(totals, axis=0, keepdims=True) + jnp.zeros((16, 128), F32),
+        ],
+        axis=0,
+    )
+    factors = dot(
+        jnp.concatenate([part[:, 0:32] for part in thirds(jnp.exp2(exponents))], axis=1),
+        onehot((96, width), (0, 32, 64)).astype(BF16),
+    )
+    drow_ref[...] = factors[0:24]
+    grow_ref[...] = factors[24:48]
+    dec_all[me] = factors[48:49]
     st_ref[...] = jnp.zeros_like(st_ref)
 
     def halo_copies():
@@ -260,10 +274,9 @@
                 bcbuf[window, 128 * j : 128 * j + 128], taps[:, 128 * j : 128 * j + 128],
                 shift_ref.at[side, lanes + j],
             ).astype(BF16)
-            for j in range(2)
+            for j in range(1)
         ]
         bcs_ref[c, :, 0:128] = bcs[0]
-        bcs_ref[c, :, 128:256] = bcs[1]
         taps = kx_ref[...].astype(F32) * 0.5
         for j in range(0, lanes, 2):
             wide = slice(128 * j, 128 * j + 256)
@@ -341,7 +354,7 @@
         one_copy(seq_peer(k), me).start()
         return 0
 
-    lax.fori_loop(1, nseq, send_one, 0)
+    lax.fori_loop(1, nseq, send_one, 0, unroll=True)
 
     def second_round():
         def arrived(k, _):
@@ -359,57 +372,66 @@
                 send2[k, e] = acc.astype(BF16)
                 return dec_all[k, :, cols] * acc + recv1[k, e].astype(F32)
 
-            lax.fori_loop(0, nseq, scan, jnp.zeros((8, half), F32))
+            lax.fori_loop(0, nseq, scan, jnp.zeros((8, half), F32), unroll=8)
         recv2[me] = send2[me]
 
         def send_two(k, _):
             two_copy(seq_peer(k), me).start()
             return 0
 
-        lax.fori_loop(1, nseq, send_two, 0)
+        lax.fori_loop(1, nseq, send_two, 0, unroll=True)
 
     lane = lax.broadcasted_iota(jnp.int32, (Q, 128), 1)
     left = jnp.where(lane < HP, 1.0, 0.0).astype(BF16)
     right = jnp.where(lane < HP, 0.0, 1.0).astype(BF16)
+    first_head = lax.broadcasted_iota(jnp.int32, (1, 128), 1) < HP
     lower = lax.broadcasted_iota(jnp.int32, (Q, Q), 0) >= lax.broadcasted_iota(jnp.int32, (Q, Q), 1)
 
-    def phase_b(c, _):
-        drow = drow_ref[pl.ds(c, 1), :]
-        at = pl.ds(pl.multiple_of(c * Q, Q), Q)
-        scores = jnp.where(lower, dot(bcs_ref[c, :, 128:256], bcs_ref[c, :, 0:128], 1, 1), 0.0)
-        for j in range(lanes):
-            cols = slice(128 * j, 128 * j + 128)
-            weights = []
-            for h in (2 * j, 2 * j + 1):
-                gap = acol_ref[c, :, h : h + 1] - brow_ref[pl.ds(16 * c + h, 1), :]
-                weights.append((scores * jnp.exp2(jnp.minimum(gap, 0.0))).astype(BF16))
-            xs = xs_ref[c, :, cols]
-            pair = jnp.concatenate([xs * left, xs * right], axis=0)
-            intra = dot(jnp.concatenate(weights, axis=1), pair)
-            skip = jnp.where(lane < HP, skip_ref[2 * j], skip_ref[2 * j + 1])
-            state = st_ref[:, cols]
-            st_ref[:, cols] = drow[:, cols] * state + u_ref[c, :, cols]
-            if j % 2 == 0:
-                wide = slice(128 * j, 128 * j + 256)
-                decays = dot(colb_ref[c], ohe_ref[:, wide])
-                before = []
-            before.append(state.astype(BF16))
-            y = intra + skip * xs.astype(F32)
-            if j % 2 == 1:
-                carried = dot(bcs_ref[c, :, 128:256], jnp.concatenate(before, axis=1)) * decays
-                y_ref[c, :, 128 * j - 128 : 128 * j] = held + carried[:, :128]
-                y_ref[c, :, cols] = y + carried[:, 128:]
-            held = y
-            h = (gbuf[at, cols] * jnp.asarray(0.5, BF16)).astype(F32)
-            sg_ref[c, :, cols] = h + h * jnp.tanh(h)
+    def phase_b(i, _):
+        both = pl.ds(2 * i, 2)
+        all_columns = colb_ref[both].reshape(2 * Q, 128)
+        scores, drow = [], []
+        for t in range(2):
+            c = 2 * i + t
+            bcs_ref[c, :, 128:256] = conv_half_silu(
+                bcbuf[pl.ds(pl.multiple_of(c * Q, Q), Q + HALO), 128:256],
+                kbc_ref[:, 128:256].astype(F32) * 0.5,
+                shift_ref.at[t, lanes + 1],
+            ).astype(BF16)
+            scores.append(
+                jnp.where(lower, dot(bcs_ref[c, :, 128:256], bcs_ref[c, :, 0:128], 1, 1), 0.0)
+            )
+            drow.append(drow_ref[pl.ds(c, 1), :])
+        for j in range(0, lanes, 2):
+            wide = slice(128 * j, 128 * j + 256)
+            decays = dot(all_columns, ohe_ref[:, wide])
+            for t in range(2):
+                c = 2 * i + t
+                at = pl.ds(pl.multiple_of(c * Q, Q), Q)
+                state = st_ref[:, wide]
+                st_ref[:, wide] = drow[t][:, wide] * state + u_ref[c, :, wide]
+                carried = dot(bcs_ref[c, :, 128:256], state.astype(BF16)) * decays[Q * t : Q * t + Q]
+                for k in range(2):
+                    cols = slice(128 * (j + k), 128 * (j + k) + 128)
+                    weights = []
+                    for h in (2 * (j + k), 2 * (j + k) + 1):
+                        gap = acol_ref[c, :, h : h + 1] - brow_ref[pl.ds(16 * c + h, 1), :]
+                        weights.append((scores[t] * jnp.exp2(jnp.minimum(gap, 0.0))).astype(BF16))
+                    xs = xs_ref[c, :, cols]
+                    pair = jnp.concatenate([xs * left, xs * right], axis=0)
+                    intra = dot(jnp.concatenate(weights, axis=1), pair)
+                    skip = jnp.where(first_head, skip_ref[2 * (j + k)], skip_ref[2 * (j + k) + 1])
+                    y_ref[c, :, cols] = intra + skip * xs.astype(F32) + carried[:, 128 * k : 128 * k + 128]
+                    h = gbuf[at, cols].astype(F32) * 0.5
+                    sg_ref[c, :, cols] = h + h * jnp.tanh(h)
         return 0
 
     gate_copy.wait()
     st_ref[...] = jnp.zeros_like(st_ref)
-    split = nc // 4 * 2
-    lax.fori_loop(0, split, phase_b, 0, unroll=UNROLL_B)
+    split = nc // 4
+    lax.fori_loop(0, split, phase_b, 0)
     second_round()
-    lax.fori_loop(split, nc, phase_b, 0, unroll=UNROLL_B)
+    lax.fori_loop(split, nc // 2, phase_b, 0)
 
     def arrived_two(k, _):
         peer = seq_peer(k)
@@ -456,7 +478,7 @@
             ss_copy(head_peer(k), mz, g).start()
             return 0
 
-        lax.fori_loop(1, nhead, send_ss, 0)
+        lax.fori_loop(1, nhead, send_ss, 0, unroll=True)
 
     eye = lax.broadcasted_iota(jnp.int32, (Q, Q), 0) == lax.broadcasted_iota(jnp.int32, (Q, Q), 1)
     gain = gain_ref[...].reshape(1, width)
@@ -473,16 +495,6 @@
             out_ref[at, cols] = (u_ref[c, :, cols] * scale * gain[:, cols]).astype(BF16)
         return 0
 
-    for g in range(len(groups)):
-
-        def arrived_ss(k, _):
-            peer = head_peer(k)
-            ss_copy(peer, peer, g).wait_recv()
-            return 0
-
-        lax.fori_loop(1, nhead, arrived_ss, 0)
-        lax.fori_loop(*groups[g], phase_d, 0, unroll=2)
-
     for copy in halo_copies():
         copy.wait_send()
 
@@ -494,6 +506,16 @@
         return 0
 
     lax.fori_loop(1, nseq, left_seq, 0)
+
+    for g in range(len(groups)):
+
+        def arrived_ss(k, _):
+            peer = head_peer(k)
+            ss_copy(peer, peer, g).wait_recv()
+            return 0
+
+        lax.fori_loop(1, nhead, arrived_ss, 0)
+        lax.fori_loop(*groups[g], phase_d, 0, unroll=2)
 
     def left_head(k, _):
         for g in range(len(groups)):
@@ -509,7 +531,7 @@
     nc = rows // Q
     per = PIECES // nseq
     half = width // 2
-    groups = 2
+    groups = 3
     vmem = pl.BlockSpec(memory_space=pltpu.VMEM)
     dma = pltpu.SemaphoreType.DMA
     return pl.pallas_call(

time: 48 us -> 45.2 us (0.942)
  Pallas kernels: 46 us -> 43.2 us
    pallas_call x1, Pallas kernels: 46 us -> 43.2 us  [per_device(): pl.pallas_call(functools.partial(kernel, nseq, nhead), out_shape=pltpu.VM...]
where the time goes in v3:
time: 45.2 us; the launch traced here: 45.1 us
  Pallas kernels  43.2 us (96%)
  local copies, waits for them, and re-layouts  1.93 us (4%)
    pallas_call x1, Pallas kernels, per_device(): pl.pallas_call(functools.partial(kernel, nseq, nhead), out_shape=pltpu.VM...  43.2 us
    unnamed x1, local copies, waits for them, and re-layouts  1.93 us

profile of v3, /device:TPU:1, one launch (start us, length us, event | category | flops | bytes accessed | tf_op | source)
XLA Modules:
  0.0 45.1 jit_solution(8997766412017508889)
XLA Ops:
  0.0 43.2 %mamba.1 = bf16[2560,768]{1,0:T(8,128)(2,1)S(1)} custom-call(bf16[2560,768]{1,0:T(8,128)(2,1)} %x_hbm.1, bf16[2560,256]{1,0:T(8,128)(2,1)} %bc_hbm.1, bf16[2560,768]{1,0:T(8,128)(2,1)} %gate_hbm.1, f32[12,2560]{1,0:T(8,128)} %ld_hbm.1, f32[12,2560]{1,0:T(8,128)} %dt_hbm.1, bf16[4,768]{1,0:T(4,128)(2,1)} %kx_hbm.1, bf16[4,256]{1,0:T(4,128)(2,1)} %kbc_hbm.1, ...), custom_call_target="tpu_custom_call" | custom-call | tf_op jit(solution)/shard_map/mamba/pallas_call | solution.py:537
  43.2 1.9 %copy.11 = bf16[2560,768]{1,0:T(8,128)(2,1)} copy(bf16[2560,768]{1,0:T(8,128)(2,1)S(1)} %mamba.1) | data formatting | bytes 7864320

commit v4 on v3

--- a/solution.py
+++ b/solution.py
@@ -14,7 +14,7 @@
 HALO = 16
 PIECES = 32
 IN_PIECES = 5
-GREET_PIECE = 2
+GREET_PIECE = 1
 VMEM_LIMIT = 56 * 1024 * 1024
 LOG2E = 1.4426950408889634
 F32 = jnp.float32
@@ -351,7 +351,7 @@
         )
 
     def send_one(k, _):
-        one_copy(seq_peer(k), me).start()
+        one_copy(seq_peer(lax.rem(k + nseq // 4, nseq - 1) + 1), me).start()
         return 0
 
     lax.fori_loop(1, nseq, send_one, 0, unroll=True)
@@ -376,7 +376,7 @@
         recv2[me] = send2[me]
 
         def send_two(k, _):
-            two_copy(seq_peer(k), me).start()
+            two_copy(seq_peer(lax.rem(k + nseq // 4, nseq - 1) + 1), me).start()
             return 0
 
         lax.fori_loop(1, nseq, send_two, 0, unroll=True)

time: 45.2 us -> 44.8 us (level)
  no operation moved by 1% of the time
where the time goes in v4:
time: 44.8 us; the launch traced here: 44.7 us
  Pallas kernels  42.8 us (96%)
  local copies, waits for them, and re-layouts  1.93 us (4%)
    pallas_call x1, Pallas kernels, per_device(): pl.pallas_call(functools.partial(kernel, nseq, nhead), out_shape=pltpu.VM...  42.8 us
    unnamed x1, local copies, waits for them, and re-layouts  1.93 us

profile of v4, /device:TPU:1, one launch (start us, length us, event | category | flops | bytes accessed | tf_op | source)
XLA Modules:
  0.0 44.7 jit_solution(4195617671186673459)
XLA Ops:
  0.0 42.8 %mamba.1 = bf16[2560,768]{1,0:T(8,128)(2,1)S(1)} custom-call(bf16[2560,768]{1,0:T(8,128)(2,1)} %x_hbm.1, bf16[2560,256]{1,0:T(8,128)(2,1)} %bc_hbm.1, bf16[2560,768]{1,0:T(8,128)(2,1)} %gate_hbm.1, f32[12,2560]{1,0:T(8,128)} %ld_hbm.1, f32[12,2560]{1,0:T(8,128)} %dt_hbm.1, bf16[4,768]{1,0:T(4,128)(2,1)} %kx_hbm.1, bf16[4,256]{1,0:T(4,128)(2,1)} %kbc_hbm.1, ...), custom_call_target="tpu_custom_call" | custom-call | tf_op jit(solution)/shard_map/mamba/pallas_call | solution.py:537
  42.8 1.9 %copy.11 = bf16[2560,768]{1,0:T(8,128)(2,1)} copy(bf16[2560,768]{1,0:T(8,128)(2,1)S(1)} %mamba.1) | data formatting | bytes 7864320
